TPU v7x, 32 devices: a whole 2x2x4 slice. The times are simulated.
32 devices in a mesh: dp: 8 (over z, y), tensor: 4 (over x, core).
Axes of the slice: x: 2, y: 2, z: 4, core: 2. Of those that a mesh axis runs over, the one named last changes fastest.
Arguments:
- tokens: bfloat16 [16384, 768], P(('dp', 'tensor')), may hold values from -6 to 6
- cotangent: bfloat16 [16384, 768], P(('dp', 'tensor')), may hold values from -6 to 6
- segment_ids: int32 [8, 2048], P('dp'), may hold values from 0 to 7, never falling along the last dimension, each value on 1 to 512 neighbouring positions
- ln1_gain: bfloat16 [768], P('dp'), may hold values from 0.5 to 1.5
- ln1_bias: bfloat16 [768], P('dp'), may hold values from -3 to 3
- w_query: bfloat16 [768, 768], P('dp', 'tensor'), may hold values from -0.3125 to 0.3125
- query_bias: bfloat16 [768], P('dp'), may hold values from -3 to 3
- w_key: bfloat16 [768, 768], P('dp', 'tensor'), may hold values from -0.3125 to 0.3125
- w_value: bfloat16 [768, 768], P('dp', 'tensor'), may hold values from -0.21875 to 0.21875
- value_bias: bfloat16 [768], P('dp'), may hold values from -3 to 3
- w_out: bfloat16 [768, 768], P('tensor', 'dp'), may hold values from -0.625 to 0.625
- out_bias: bfloat16 [768], P('dp'), may hold values from -3 to 3
- ln2_gain: bfloat16 [768], P('dp'), may hold values from 0.5 to 1.5
- ln2_bias: bfloat16 [768], P('dp'), may hold values from -3 to 3
- w_in: bfloat16 [768, 3072], P('dp', 'tensor'), may hold values from -0.21875 to 0.21875
- in_bias: bfloat16 [3072], P('dp'), may hold values from -3 to 3
- w_back: bfloat16 [3072, 768], P('tensor', 'dp'), may hold values from -0.15625 to 0.15625
- back_bias: bfloat16 [768], P('dp'), may hold values from -3 to 3
Outputs:
- output: bfloat16 [16384, 768], P(('dp', 'tensor'))
- grad_tokens: float32 [16384, 768], P(('dp', 'tensor'))
- grad_ln1_gain: float32 [768], P('dp')
- grad_ln1_bias: float32 [768], P('dp')
- grad_w_query: float32 [768, 768], P('dp', 'tensor')
- grad_query_bias: float32 [768], P('dp')
- grad_w_key: float32 [768, 768], P('dp', 'tensor')
- grad_w_value: float32 [768, 768], P('dp', 'tensor')
- grad_value_bias: float32 [768], P('dp')
- grad_w_out: float32 [768, 768], P('tensor', 'dp')
- grad_out_bias: float32 [768], P('dp')
- grad_ln2_gain: float32 [768], P('dp')
- grad_ln2_bias: float32 [768], P('dp')
- grad_w_in: float32 [768, 3072], P('dp', 'tensor')
- grad_in_bias: float32 [3072], P('dp')
- grad_w_back: float32 [3072, 768], P('tensor', 'dp')
- grad_back_bias: float32 [768], P('dp')
Inputs may be any that keep to these rules, and one draw needn't show every extreme that they name: `segment_ids`: in each sequence the document numbers never fall; every number 0 to 7 appears, on 1 to 512 consecutive patches, and some document has exactly 512.
All inputs are finite; a program needn't handle non-finite values.
Results may differ from a plain program's by a relative error of at most 0.02.
Values may be sent and summed in bfloat16 or wider, within the bound.
A program may use at most 128 MiB of HBM per device.

v0:
```python
import math
import jax
import jax.numpy as jnp
from jax import lax
from jax.sharding import PartitionSpec as P

HEAD_DIM = 64
EPSILON = 1e-12


def layer_norm(values, gain, shift):
    center = values - jnp.mean(values, axis=-1, keepdims=True)
    spread = jnp.mean(center * center, axis=-1, keepdims=True)
    return center * lax.rsqrt(spread + EPSILON) * gain + shift


def gelu_exact(values):
    return jax.nn.gelu(values, approximate=False)


def contract_rows(left, right):
    return lax.dot_general(
        left, right, (((0,), (0,)), ((), ())), preferred_element_type=jnp.float32
    )


def contract_cols(left, right):
    return lax.dot_general(
        left, right, (((1,), (1,)), ((), ())), preferred_element_type=jnp.float32
    )


def place_slice(length, piece, start):
    return lax.dynamic_update_slice_in_dim(jnp.zeros((length,), jnp.float32), piece, start, 0)


def per_device(
    tokens,
    cotangent,
    segment_ids,
    ln1_gain,
    ln1_bias,
    w_query,
    query_bias,
    w_key,
    w_value,
    value_bias,
    w_out,
    out_bias,
    ln2_gain,
    ln2_bias,
    w_in,
    in_bias,
    w_back,
    back_bias,
):
    f32 = jnp.float32
    bf16 = jnp.bfloat16
    index = lax.axis_index("tensor")
    (
        gain_one,
        shift_one,
        full_query,
        qbias_all,
        full_key,
        full_value,
        vbias_all,
        full_out,
        obias_all,
        gain_two,
        shift_two,
        full_in,
        ibias_all,
        full_back,
        bbias_all,
    ) = (
        lax.all_gather(ln1_gain, "dp", axis=0, tiled=True),
        lax.all_gather(ln1_bias, "dp", axis=0, tiled=True),
        lax.all_gather(w_query, "dp", axis=0, tiled=True),
        lax.all_gather(query_bias, "dp", axis=0, tiled=True),
        lax.all_gather(w_key, "dp", axis=0, tiled=True),
        lax.all_gather(w_value, "dp", axis=0, tiled=True),
        lax.all_gather(value_bias, "dp", axis=0, tiled=True),
        lax.all_gather(w_out, "dp", axis=1, tiled=True),
        lax.all_gather(out_bias, "dp", axis=0, tiled=True),
        lax.all_gather(ln2_gain, "dp", axis=0, tiled=True),
        lax.all_gather(ln2_bias, "dp", axis=0, tiled=True),
        lax.all_gather(w_in, "dp", axis=0, tiled=True),
        lax.all_gather(in_bias, "dp", axis=0, tiled=True),
        lax.all_gather(w_back, "dp", axis=1, tiled=True),
        lax.all_gather(back_bias, "dp", axis=0, tiled=True),
    )
    width = tokens.shape[1]
    head_width = full_query.shape[1]
    hidden_width = full_in.shape[1]
    unit_total = ibias_all.shape[0]
    local_heads = head_width // HEAD_DIM
    scale = HEAD_DIM ** (-0.5)
    gain_one = gain_one.astype(f32)
    shift_one = shift_one.astype(f32)
    gain_two = gain_two.astype(f32)
    shift_two = shift_two.astype(f32)
    query_shift = lax.dynamic_slice_in_dim(qbias_all, index * head_width, head_width).astype(f32)
    value_shift = lax.dynamic_slice_in_dim(vbias_all, index * head_width, head_width).astype(f32)
    unit_shift = lax.dynamic_slice_in_dim(ibias_all, index * hidden_width, hidden_width).astype(f32)
    inputs = tokens.astype(f32)
    act_one = layer_norm(inputs, gain_one, shift_one).astype(bf16)
    group_one = lax.all_gather(act_one, "tensor", axis=0, tiled=True)
    merged = jnp.concatenate([full_query, full_key, full_value], axis=1)
    mixed = jnp.dot(group_one, merged, preferred_element_type=f32)
    group = mixed.shape[0]
    seq_count = segment_ids.shape[0]
    seq_len = segment_ids.shape[1]
    query = (mixed[:, :head_width] + query_shift).astype(bf16).reshape(group, local_heads, HEAD_DIM)
    keys = (
        mixed[:, head_width : 2 * head_width]
        .astype(bf16)
        .reshape(seq_count, seq_len, local_heads, HEAD_DIM)
    )
    values = (
        (mixed[:, 2 * head_width :] + value_shift)
        .astype(bf16)
        .reshape(seq_count, seq_len, local_heads, HEAD_DIM)
    )
    block = math.gcd(512, seq_len)
    per_seq = seq_len // block
    block_count = group // block

    def block_scores(number):
        sequence = number // per_seq
        begin = number * block
        offset = begin - sequence * seq_len
        query_block = lax.dynamic_slice_in_dim(query, begin, block, 0)
        key_seq = lax.dynamic_index_in_dim(keys, sequence, 0, keepdims=False)
        value_seq = lax.dynamic_index_in_dim(values, sequence, 0, keepdims=False)
        doc_all = lax.dynamic_index_in_dim(segment_ids, sequence, 0, keepdims=False)
        doc_rows = lax.dynamic_slice_in_dim(doc_all, offset, block, 0)
        raw = jnp.einsum("qhd,khd->hqk", query_block, key_seq, preferred_element_type=f32)
        same = (doc_rows[:, None] == doc_all[None, :])[None]
        scores = jnp.where(same, raw * scale, -1000000000.0)
        return (scores, query_block, key_seq, value_seq, begin, sequence)

    def forward_block(number):
        scores, query_block, key_seq, value_seq, begin, sequence = block_scores(number)
        top = jnp.max(scores, axis=-1, keepdims=True)
        expo = jnp.exp(scores - top)
        denom = jnp.sum(expo, axis=-1, keepdims=True)
        weights = (expo / denom).astype(bf16)
        result = jnp.einsum("hqk,khd->qhd", weights, value_seq, preferred_element_type=f32)
        return (
            result.reshape(block, head_width).astype(bf16),
            top[..., 0] + jnp.log(denom[..., 0]),
        )

    context_blocks, lse_all = lax.map(forward_block, jnp.arange(block_count))
    context = context_blocks.reshape(group, head_width)
    attn_part = jnp.dot(context, full_out, preferred_element_type=f32).astype(bf16)
    attn_sum = lax.psum_scatter(attn_part, "tensor", scatter_dimension=0, tiled=True).astype(
        jnp.float32
    )
    middle = inputs + attn_sum + obias_all.astype(f32)
    act_two = layer_norm(middle, gain_two, shift_two).astype(bf16)
    group_two = lax.all_gather(act_two, "tensor", axis=0, tiled=True)
    pre = jnp.dot(group_two, full_in, preferred_element_type=f32) + unit_shift
    hidden = gelu_exact(pre).astype(bf16)
    mlp_part = jnp.dot(hidden, full_back, preferred_element_type=f32).astype(bf16)
    mlp_sum = lax.psum_scatter(mlp_part, "tensor", scatter_dimension=0, tiled=True).astype(
        jnp.float32
    )
    result = middle + mlp_sum + bbias_all.astype(f32)
    output = result.astype(bf16)
    back_query, back_key, back_value, back_out, back_in, back_back = (
        lax.all_gather(w_query, "dp", axis=0, tiled=True),
        lax.all_gather(w_key, "dp", axis=0, tiled=True),
        lax.all_gather(w_value, "dp", axis=0, tiled=True),
        lax.all_gather(w_out, "dp", axis=1, tiled=True),
        lax.all_gather(w_in, "dp", axis=0, tiled=True),
        lax.all_gather(w_back, "dp", axis=1, tiled=True),
    )
    merged_back = jnp.concatenate([back_query, back_key, back_value], axis=1)
    upstream = cotangent.astype(f32)
    back_bias_term = jnp.sum(upstream, axis=0)
    cot_rows = lax.all_gather(cotangent, "tensor", axis=0, tiled=True)
    grad_w_back = contract_rows(hidden, cot_rows)
    grad_hidden = contract_cols(cot_rows, back_back)
    gelu_out, gelu_pull = jax.vjp(gelu_exact, pre)
    grad_pre = gelu_pull(grad_hidden)[0]
    unit_term = jnp.sum(grad_pre, axis=0)
    pre_low = grad_pre.astype(bf16)
    grad_w_in = contract_rows(group_two, pre_low)
    grad_norm_two = lax.psum_scatter(
        contract_cols(pre_low, back_in).astype(jnp.bfloat16),
        "tensor",
        scatter_dimension=0,
        tiled=True,
    ).astype(jnp.float32)
    norm_out, norm_pull = jax.vjp(layer_norm, middle, gain_two, shift_two)
    grad_mid_norm, ln2_gain_term, ln2_bias_term = norm_pull(grad_norm_two)
    grad_middle = upstream + grad_mid_norm
    out_bias_term = jnp.sum(grad_middle, axis=0)
    middle_low = grad_middle.astype(bf16)
    middle_rows = lax.all_gather(middle_low, "tensor", axis=0, tiled=True)
    grad_w_out = contract_rows(context, middle_rows)
    grad_context = (
        contract_cols(middle_rows, back_out).astype(bf16).reshape(group, local_heads, HEAD_DIM)
    )

    def backward_block(carry, number):
        keys_acc, values_acc = carry
        scores, query_block, key_seq, value_seq, begin, sequence = block_scores(number)
        lse = lax.dynamic_index_in_dim(lse_all, number, 0, keepdims=False)
        probs = jnp.exp(scores - lse[:, :, None])
        weights = probs.astype(bf16)
        upstream_block = lax.dynamic_slice_in_dim(grad_context, begin, block, 0)
        grad_weights = jnp.einsum(
            "qhd,khd->hqk", upstream_block, value_seq, preferred_element_type=f32
        )
        delta = jnp.sum(grad_weights * probs, axis=-1, keepdims=True)
        grad_raw = (probs * (grad_weights - delta) * scale).astype(bf16)
        query_part = jnp.einsum("hqk,khd->qhd", grad_raw, key_seq, preferred_element_type=f32)
        key_part = jnp.einsum("hqk,qhd->khd", grad_raw, query_block, preferred_element_type=f32)
        value_part = jnp.einsum("hqk,qhd->khd", weights, upstream_block, preferred_element_type=f32)
        keys_acc = lax.dynamic_update_index_in_dim(
            keys_acc,
            lax.dynamic_index_in_dim(keys_acc, sequence, 0, keepdims=False) + key_part,
            sequence,
            0,
        )
        values_acc = lax.dynamic_update_index_in_dim(
            values_acc,
            lax.dynamic_index_in_dim(values_acc, sequence, 0, keepdims=False) + value_part,
            sequence,
            0,
        )
        return ((keys_acc, values_acc), query_part)

    empty = jnp.zeros((seq_count, seq_len, local_heads, HEAD_DIM), f32)
    (grad_keys, grad_values), query_parts = lax.scan(
        backward_block, (empty, empty), jnp.arange(block_count)
    )
    grad_query = query_parts.reshape(group, head_width)
    grad_keys = grad_keys.reshape(group, head_width)
    grad_values = grad_values.reshape(group, head_width)
    query_term = jnp.sum(grad_query, axis=0)
    value_term = jnp.sum(grad_values, axis=0)
    grad_lows = jnp.concatenate([grad_query, grad_keys, grad_values], axis=1).astype(bf16)
    grad_merged = contract_rows(group_one, grad_lows)
    grad_w_query = grad_merged[:, :head_width]
    grad_w_key = grad_merged[:, head_width : 2 * head_width]
    grad_w_value = grad_merged[:, 2 * head_width :]
    grad_norm_one = lax.psum_scatter(
        contract_cols(grad_lows, merged_back).astype(jnp.bfloat16),
        "tensor",
        scatter_dimension=0,
        tiled=True,
    ).astype(jnp.float32)
    first_out, first_pull = jax.vjp(layer_norm, inputs, gain_one, shift_one)
    grad_in_norm, ln1_gain_term, ln1_bias_term = first_pull(grad_norm_one)
    grad_tokens = grad_middle + grad_in_norm
    vectors = (
        lax.psum(ln1_gain_term.astype(jnp.bfloat16), "tensor").astype(jnp.float32),
        lax.psum(ln1_bias_term.astype(jnp.bfloat16), "tensor").astype(jnp.float32),
        lax.psum(
            place_slice(width, query_term, index * head_width).astype(jnp.bfloat16), "tensor"
        ).astype(jnp.float32),
        lax.psum(
            place_slice(width, value_term, index * head_width).astype(jnp.bfloat16), "tensor"
        ).astype(jnp.float32),
        lax.psum(out_bias_term.astype(jnp.bfloat16), "tensor").astype(jnp.float32),
        lax.psum(ln2_gain_term.astype(jnp.bfloat16), "tensor").astype(jnp.float32),
        lax.psum(ln2_bias_term.astype(jnp.bfloat16), "tensor").astype(jnp.float32),
        lax.psum(
            place_slice(unit_total, unit_term, index * hidden_width).astype(jnp.bfloat16), "tensor"
        ).astype(jnp.float32),
        lax.psum(back_bias_term.astype(jnp.bfloat16), "tensor").astype(jnp.float32),
    )
    (
        grad_w_query,
        grad_w_key,
        grad_w_value,
        grad_w_out,
        grad_w_in,
        grad_w_back,
        grad_ln1_gain,
        grad_ln1_bias,
        grad_query_bias,
        grad_value_bias,
        grad_out_bias,
        grad_ln2_gain,
        grad_ln2_bias,
        grad_in_bias,
        grad_back_bias,
    ) = (
        lax.psum_scatter(grad_w_query, "dp", scatter_dimension=0, tiled=True),
        lax.psum_scatter(grad_w_key, "dp", scatter_dimension=0, tiled=True),
        lax.psum_scatter(grad_w_value, "dp", scatter_dimension=0, tiled=True),
        lax.psum_scatter(grad_w_out, "dp", scatter_dimension=1, tiled=True),
        lax.psum_scatter(grad_w_in, "dp", scatter_dimension=0, tiled=True),
        lax.psum_scatter(grad_w_back, "dp", scatter_dimension=1, tiled=True),
        lax.psum_scatter(vectors[0], "dp", scatter_dimension=0, tiled=True),
        lax.psum_scatter(vectors[1], "dp", scatter_dimension=0, tiled=True),
        lax.psum_scatter(vectors[2], "dp", scatter_dimension=0, tiled=True),
        lax.psum_scatter(vectors[3], "dp", scatter_dimension=0, tiled=True),
        lax.psum_scatter(vectors[4], "dp", scatter_dimension=0, tiled=True),
        lax.psum_scatter(vectors[5], "dp", scatter_dimension=0, tiled=True),
        lax.psum_scatter(vectors[6], "dp", scatter_dimension=0, tiled=True),
        lax.psum_scatter(vectors[7], "dp", scatter_dimension=0, tiled=True),
        lax.psum_scatter(vectors[8], "dp", scatter_dimension=0, tiled=True),
    )
    return (
        output,
        grad_tokens,
        grad_ln1_gain,
        grad_ln1_bias,
        grad_w_query,
        grad_query_bias,
        grad_w_key,
        grad_w_value,
        grad_value_bias,
        grad_w_out,
        grad_out_bias,
        grad_ln2_gain,
        grad_ln2_bias,
        grad_w_in,
        grad_in_bias,
        grad_w_back,
        grad_back_bias,
    )


def solution(mesh):
    return jax.shard_map(
        per_device,
        mesh=mesh,
        in_specs=(
            P(("dp", "tensor"), None),
            P(("dp", "tensor"), None),
            P("dp", None),
            P("dp"),
            P("dp"),
            P("dp", "tensor"),
            P("dp"),
            P("dp", "tensor"),
            P("dp", "tensor"),
            P("dp"),
            P("tensor", "dp"),
            P("dp"),
            P("dp"),
            P("dp"),
            P("dp", "tensor"),
            P("dp"),
            P("tensor", "dp"),
            P("dp"),
        ),
        out_specs=(
            P(("dp", "tensor"), None),
            P(("dp", "tensor"), None),
            P("dp"),
            P("dp"),
            P("dp", "tensor"),
            P("dp"),
            P("dp", "tensor"),
            P("dp", "tensor"),
            P("dp"),
            P("tensor", "dp"),
            P("dp"),
            P("dp"),
            P("dp"),
            P("dp", "tensor"),
            P("dp"),
            P("tensor", "dp"),
            P("dp"),
        ),
        check_vma=False,
    )
```

profile of v0, /device:TPU:0, one launch (start us, length us, event | category | flops | bytes accessed | tf_op | source)
XLA Modules:
  0.0 1247.8 jit_solution(12022204815762069830)
XLA Ops:
  19.7 39.5 %all-reduce.18 = (bf16[768]{0:T(1024)(128)(2,1)S(1)}, bf16[768]{0:T(1024)(128)(2,1)S(1)}, bf16[768]{0:T(1024)(128)(2,1)S(1)}, bf16[768]{0:T(1024)(128)(2,1)S(1)}...) all-reduce(bf16[768]{0:T(1024)(128)(2,1)S(1)} %dynamic-update-slice, ...), channel_id=1, replica_groups=mesh['dp'=8,'tensor'=4] {'dp'}, use_global_device_ids=true, to_apply=%add.1 | all-reduce | flops 6144 | bytes 24576
  62.5 31.0 %all_gather.71 = bf16[192,768]{0,1:T(8,128)(2,1)S(1)} all-gather(bf16[192,96]{0,1:T(8,128)(2,1)S(1)} %copy.44), channel_id=1, replica_groups=mesh['dp'=8,'tensor'=4] {'dp'}, dimensions={1}, use_global_device_ids=true | all-gather | bytes 331776 | tf_op jit(solution)/shard_map/all_gather | solution.py:84
  93.5 31.0 %all_gather.66 = bf16[768,192]{1,0:T(8,128)(2,1)S(1)} all-gather(bf16[96,192]{1,0:T(8,128)(2,1)S(1)} %copy-done.36), channel_id=1, replica_groups=mesh['dp'=8,'tensor'=4] {'dp'}, dimensions={0}, use_global_device_ids=true | all-gather | bytes 331776 | tf_op jit(solution)/shard_map/all_gather | solution.py:79
  124.5 31.0 %all_gather.67 = bf16[768,192]{1,0:T(8,128)(2,1)S(1)} all-gather(bf16[96,192]{1,0:T(8,128)(2,1)S(1)} %copy-done.37), channel_id=1, replica_groups=mesh['dp'=8,'tensor'=4] {'dp'}, dimensions={0}, use_global_device_ids=true | all-gather | bytes 331776 | tf_op jit(solution)/shard_map/all_gather | solution.py:81
  155.5 31.1 %all_gather.68 = bf16[768,192]{1,0:T(8,128)(2,1)S(1)} all-gather(bf16[96,192]{1,0:T(8,128)(2,1)S(1)} %copy-done.38), channel_id=1, replica_groups=mesh['dp'=8,'tensor'=4] {'dp'}, dimensions={0}, use_global_device_ids=true | all-gather | bytes 331776 | tf_op jit(solution)/shard_map/all_gather | solution.py:82
  191.6 98.7 %while.30 = (s32[]{:T(128)}, bf16[4,512,192]{1,2,0:T(8,128)(2,1)}, f32[4,3,512]{2,1,0:T(4,128)S(1)}, s32[4]{0:T(128)S(1)}, s32[1,2048]{1,0:T(1,128)S(1)}, /*inde...) while((s32[]{:T(128)}, bf16[4,512,192]{1,2,0:T(8,128)(2,1)}, ...), condition=%wide.region_5.6_spmd, body=%wide.region_2.5_spmd.sunk | while | flops 844200448 | bytes 44372400 | solution.py:155
  202.1 6.8 fusion.178
  208.8 6.7 fusion.179
  226.8 6.8 fusion.178
  233.5 6.7 fusion.179
  251.4 6.8 fusion.178
  258.2 6.7 fusion.179
  276.1 6.8 fusion.178
  282.9 6.7 fusion.179
  296.1 34.7 %reduce-scatter.19.cloned.1.call-done = bf16[512,768]{1,0:T(8,128)(2,1)} async-done(((bf16[2048,768]{1,0:T(8,128)(2,1)}), bf16[512,768]{1,0:T(8,128)(2,1)}) %reduce-scatter.19.cloned.1.call-update) | async-done | bytes 786448 | tf_op jit(solution)/shard_map/reduce_scatter | solution.py:158
  336.7 26.4 %all-gather = bf16[8,1,384]{2,1,0:T(2,128)(2,1)S(1)} all-gather(bf16[1,1,384]{2,1,0:T(2,128)(2,1)S(1)} %reshape.282), channel_id=1, replica_groups=mesh['dp'=8,'tensor'=4] {'dp'}, dimensions={0}, use_global_device_ids=true | all-gather | bytes 6912 | tf_op jit(solution)/shard_map/all_gather | solution.py:89
  366.1 7.6 fusion.135
  373.6 36.3 %all-gather.14.cloned.1.call-done = bf16[768,768]{0,1:T(8,128)(2,1)} async-done(((bf16[768,96]{0,1:T(8,128)(2,1)}), bf16[768,768]{0,1:T(8,128)(2,1)}) %all-gather.14.cloned.1.call-update) | async-done | bytes 1179664 | tf_op jit(solution)/shard_map/all_gather | solution.py:90
  409.9 28.5 %all-gather.16.cloned.1.call-done = bf16[2048,768]{1,0:T(8,128)(2,1)} async-done(((bf16[512,768]{1,0:T(8,128)(2,1)}), bf16[2048,768]{1,0:T(8,128)(2,1)}) %all-gather.16.cloned.1.call-update) | async-done | bytes 3145744 | tf_op jit(solution)/shard_map/all_gather | solution.py:183
  438.5 20.5 %fusion.128 = (bf16[768]{0:T(1024)(128)(2,1)}, bf16[2048,768]{1,0:T(8,128)(2,1)S(1)}, f32[2048,768]{1,0:T(8,128)}) fusion(f32[2048,768]{1,0:T(8,128)} %fusion.135, f32[768]{0:T(1024)S(1)} %dynamic-slice_convert_fusion, bf16[2048,768]{1,0:T(8,128)(2,1)} %all-gather.16.cloned.1.call-done, bf16[768,768]{0,1:T(8,128)(2,1)} %all-gather.14.cloned.1.call-done), kind=kOutput, calls=%fused_computation.153 | convolution fusion | flops 2532310272 | bytes 20058624 | tf_op jit(solution)/shard_map/dot_general | solution.py:28
  476.8 26.1 %reduce-scatter.23.cloned.1.call-done = bf16[512,768]{1,0:T(8,128)(2,1)} async-done(((bf16[2048,768]{1,0:T(8,128)(2,1)}), bf16[512,768]{1,0:T(8,128)(2,1)}) %reduce-scatter.23.cloned.1.call-update) | async-done | bytes 786448 | tf_op jit(solution)/shard_map/reduce_scatter | solution.py:191
  507.4 35.9 %reduce-scatter.21.cloned.1.call-done = bf16[512,768]{1,0:T(8,128)(2,1)} async-done(((bf16[2048,768]{1,0:T(8,128)(2,1)}), bf16[512,768]{1,0:T(8,128)(2,1)}) %reduce-scatter.21.cloned.1.call-update) | async-done | bytes 786448 | tf_op jit(solution)/shard_map/reduce_scatter | solution.py:167
  549.5 28.4 %all-gather.18.cloned.1.call-done = bf16[2048,768]{1,0:T(8,128)(2,1)} async-done(((bf16[512,768]{1,0:T(8,128)(2,1)}), bf16[2048,768]{1,0:T(8,128)(2,1)}) %all-gather.18.cloned.1.call-update) | async-done | bytes 3145744 | tf_op jit(solution)/shard_map/all_gather | solution.py:202
  588.9 258.0 %while.31 = (s32[]{:T(128)}, f32[1,2048,3,64]{1,3,2,0:T(8,128)}, f32[1,2048,3,64]{1,3,2,0:T(8,128)}, f32[4,512,3,64]{1,3,2,0:T(8,128)}, s32[4]{0:T(128)S(1)}, /*...) while((s32[]{:T(128)}, f32[1,2048,3,64]{1,3,2,0:T(8,128)}, ...), condition=%wide.region_15.16_spmd, body=%wide.region_13.15_spmd.sunk | while | flops 2096897024 | bytes 208079408 | solution.py:238
  596.7 7.2 fusion.193
  604.0 6.3 fusion.190
  610.3 20.9 %fusion.194 = f32[4,512,3,64]{1,3,2,0:T(8,128)} fusion(f32[4,512,3,64]{1,3,2,0:T(8,128)} %get-tuple-element.595, s32[]{:T(128)S(6)} %copy.83, f32[3,512,2048]{2,1,0:T(8,128)} %fusion.190, f32[3,512,2048]{2,1,0:T(8,128)} %copy-done, f32[3,512]{1,0:T(4,128)S(1)} %dynamic-slice_bitcast_fusion.2, pred[512,2048]{1,0:T(8,128)(4,1)S(1)} %broadcast_compare_fusion.5, ...), kind=kOutput, calls=%fused_computation.44.clone.1 | convolution fusion | flops 437259776 | bytes 53624836 | tf_op jit(solution)/shard_map/while/body/eval_jaxpr/hqk,khd->qhd/dot_general | solution.py:220
  631.2 22.6 %fusion.192 = f32[1,2048,3,64]{1,3,2,0:T(8,128)} fusion(f32[3,512,2048]{2,1,0:T(8,128)} %fusion.190, f32[3,512,2048]{2,1,0:T(8,128)} %copy-done, f32[3,512]{1,0:T(4,128)S(1)} %dynamic-slice_bitcast_fusion.2, pred[512,2048]{1,0:T(8,128)(4,1)S(1)} %broadcast_compare_fusion.5, f32[1,2048,3,64]{1,3,2,0:T(8,128)} %get-tuple-element.593, ...), kind=kOutput, calls=%fused_computation.39.clone.1 | convolution fusion | flops 437652992 | bytes 55787524 | tf_op jit(solution)/shard_map/while/body/eval_jaxpr/hqk,qhd->khd/dot_general | solution.py:221
  661.5 7.2 fusion.193
  668.7 6.3 fusion.190
  675.0 20.7 %fusion.194 = f32[4,512,3,64]{1,3,2,0:T(8,128)} fusion(f32[4,512,3,64]{1,3,2,0:T(8,128)} %get-tuple-element.595, s32[]{:T(128)S(6)} %copy.83, f32[3,512,2048]{2,1,0:T(8,128)} %fusion.190, f32[3,512,2048]{2,1,0:T(8,128)} %copy-done, f32[3,512]{1,0:T(4,128)S(1)} %dynamic-slice_bitcast_fusion.2, pred[512,2048]{1,0:T(8,128)(4,1)S(1)} %broadcast_compare_fusion.5, ...), kind=kOutput, calls=%fused_computation.44.clone.1 | convolution fusion | flops 437259776 | bytes 53624836 | tf_op jit(solution)/shard_map/while/body/eval_jaxpr/hqk,khd->qhd/dot_general | solution.py:220
  695.7 22.4 %fusion.192 = f32[1,2048,3,64]{1,3,2,0:T(8,128)} fusion(f32[3,512,2048]{2,1,0:T(8,128)} %fusion.190, f32[3,512,2048]{2,1,0:T(8,128)} %copy-done, f32[3,512]{1,0:T(4,128)S(1)} %dynamic-slice_bitcast_fusion.2, pred[512,2048]{1,0:T(8,128)(4,1)S(1)} %broadcast_compare_fusion.5, f32[1,2048,3,64]{1,3,2,0:T(8,128)} %get-tuple-element.593, ...), kind=kOutput, calls=%fused_computation.39.clone.1 | convolution fusion | flops 437652992 | bytes 55787524 | tf_op jit(solution)/shard_map/while/body/eval_jaxpr/hqk,qhd->khd/dot_general | solution.py:221
  725.8 7.2 fusion.193
  739.2 20.7 %fusion.194 = f32[4,512,3,64]{1,3,2,0:T(8,128)} fusion(f32[4,512,3,64]{1,3,2,0:T(8,128)} %get-tuple-element.595, s32[]{:T(128)S(6)} %copy.83, f32[3,512,2048]{2,1,0:T(8,128)} %fusion.190, f32[3,512,2048]{2,1,0:T(8,128)} %copy-done, f32[3,512]{1,0:T(4,128)S(1)} %dynamic-slice_bitcast_fusion.2, pred[512,2048]{1,0:T(8,128)(4,1)S(1)} %broadcast_compare_fusion.5, ...), kind=kOutput, calls=%fused_computation.44.clone.1 | convolution fusion | flops 437259776 | bytes 53624836 | tf_op jit(solution)/shard_map/while/body/eval_jaxpr/hqk,khd->qhd/dot_general | solution.py:220
  760.0 22.4 %fusion.192 = f32[1,2048,3,64]{1,3,2,0:T(8,128)} fusion(f32[3,512,2048]{2,1,0:T(8,128)} %fusion.190, f32[3,512,2048]{2,1,0:T(8,128)} %copy-done, f32[3,512]{1,0:T(4,128)S(1)} %dynamic-slice_bitcast_fusion.2, pred[512,2048]{1,0:T(8,128)(4,1)S(1)} %broadcast_compare_fusion.5, f32[1,2048,3,64]{1,3,2,0:T(8,128)} %get-tuple-element.593, ...), kind=kOutput, calls=%fused_computation.39.clone.1 | convolution fusion | flops 437652992 | bytes 55787524 | tf_op jit(solution)/shard_map/while/body/eval_jaxpr/hqk,qhd->khd/dot_general | solution.py:221
  790.1 7.2 fusion.193
  797.3 6.3 fusion.190
  803.6 20.8 %fusion.194 = f32[4,512,3,64]{1,3,2,0:T(8,128)} fusion(f32[4,512,3,64]{1,3,2,0:T(8,128)} %get-tuple-element.595, s32[]{:T(128)S(6)} %copy.83, f32[3,512,2048]{2,1,0:T(8,128)} %fusion.190, f32[3,512,2048]{2,1,0:T(8,128)} %copy-done, f32[3,512]{1,0:T(4,128)S(1)} %dynamic-slice_bitcast_fusion.2, pred[512,2048]{1,0:T(8,128)(4,1)S(1)} %broadcast_compare_fusion.5, ...), kind=kOutput, calls=%fused_computation.44.clone.1 | convolution fusion | flops 437259776 | bytes 53624836 | tf_op jit(solution)/shard_map/while/body/eval_jaxpr/hqk,khd->qhd/dot_general | solution.py:220
  824.3 22.4 %fusion.192 = f32[1,2048,3,64]{1,3,2,0:T(8,128)} fusion(f32[3,512,2048]{2,1,0:T(8,128)} %fusion.190, f32[3,512,2048]{2,1,0:T(8,128)} %copy-done, f32[3,512]{1,0:T(4,128)S(1)} %dynamic-slice_bitcast_fusion.2, pred[512,2048]{1,0:T(8,128)(4,1)S(1)} %broadcast_compare_fusion.5, f32[1,2048,3,64]{1,3,2,0:T(8,128)} %get-tuple-element.593, ...), kind=kOutput, calls=%fused_computation.39.clone.1 | convolution fusion | flops 437652992 | bytes 55787524 | tf_op jit(solution)/shard_map/while/body/eval_jaxpr/hqk,qhd->khd/dot_general | solution.py:221
  866.8 7.5 fusion.114
  887.3 9.5 reduce-scatter.25.cloned.1.call-done
  901.8 10.3 all-reduce.19
  912.1 38.8 %all-reduce.17 = (f32[768]{0:T(1024)S(1)}, f32[768]{0:T(1024)S(1)}, f32[768]{0:T(1024)S(1)}, f32[768]{0:T(1024)S(1)}, f32[768]{0:T(1024)S(1)}, /*index=5*/f32[76...) all-reduce(bf16[768]{0:T(1024)(128)(2,1)S(1)} %get-tuple-element.37, ...), channel_id=6, replica_groups=mesh['dp'=8,'tensor'=4] {'dp'}, use_global_device_ids=true, to_apply=%region_21.22.clone | all-reduce | flops 9216 | bytes 55296
  958.0 12.7 %reduce-scatter.29.cloned.1.call-done = f32[768,96]{0,1:T(8,128)} async-done(((f32[768,768]{0,1:T(8,128)}), f32[768,96]{0,1:T(8,128)}) %reduce-scatter.29.cloned.1.call-update) | async-done | bytes 294928 | tf_op jit(solution)/shard_map/reduce_scatter | solution.py:299
  970.7 72.6 %reduce-scatter.27.cloned.1.call-done = f32[96,768]{1,0:T(8,128)} async-done(((f32[768,768]{1,0:T(8,128)}), f32[96,768]{1,0:T(8,128)}) %reduce-scatter.27.cloned.1.call-update) | async-done | bytes 294928 | tf_op jit(solution)/shard_map/reduce_scatter | solution.py:298
  1043.2 65.9 %reduce-scatter.35.cloned.1.call-done = f32[96,192]{1,0:T(8,128)} async-done(((f32[768,192]{1,0:T(8,128)}), f32[96,192]{1,0:T(8,128)}) %reduce-scatter.35.cloned.1.call-update) | async-done | bytes 73744
  1109.2 65.4 %reduce-scatter.33.cloned.1.call-done = f32[96,192]{1,0:T(8,128)} async-done(((f32[768,192]{1,0:T(8,128)}), f32[96,192]{1,0:T(8,128)}) %reduce-scatter.33.cloned.1.call-update) | async-done | bytes 73744
  1174.5 65.9 %reduce-scatter.31.cloned.1.call-done = f32[96,192]{1,0:T(8,128)} async-done(((f32[768,192]{1,0:T(8,128)}), f32[96,192]{1,0:T(8,128)}) %reduce-scatter.31.cloned.1.call-update) | async-done | bytes 73744
  (297 shorter events, 166.8 us)
Async XLA Ops:
  8.0 54.3 %copy-start.39 = (bf16[192,96]{1,0:T(8,128)(2,1)S(1)}, bf16[192,96]{1,0:T(8,128)(2,1)}, u32[]{:S(2)}) copy-start(bf16[192,96]{1,0:T(8,128)(2,1)} %param.32) | copy-start | bytes 110596
  8.0 85.5 %copy-start.36 = (bf16[96,192]{1,0:T(8,128)(2,1)S(1)}, bf16[96,192]{1,0:T(8,128)(2,1)}, u32[]{:S(2)}) copy-start(bf16[96,192]{1,0:T(8,128)(2,1)} %param.27) | copy-start | bytes 110596
  8.0 116.4 %copy-start.37 = (bf16[96,192]{1,0:T(8,128)(2,1)S(1)}, bf16[96,192]{1,0:T(8,128)(2,1)}, u32[]{:S(2)}) copy-start(bf16[96,192]{1,0:T(8,128)(2,1)} %param.29) | copy-start | bytes 110596
  8.1 147.4 %copy-start.38 = (bf16[96,192]{1,0:T(8,128)(2,1)S(1)}, bf16[96,192]{1,0:T(8,128)(2,1)}, u32[]{:S(2)}) copy-start(bf16[96,192]{1,0:T(8,128)(2,1)} %param.30) | copy-start | bytes 110596
  8.1 178.5 %all-gather.8.cloned.1.call-start = ((), (), s32[]{:S(2)}) async-start(), calls=%async_computation.10 | async-start | bytes 3932160 | tf_op jit(solution)/shard_map/all_gather | solution.py:108
  9.4 52.8 %copy-start.34 = (f32[512]{0:T(512)}, f32[512]{0:T(512)S(1)}, u32[]{:S(2)}) copy-start(f32[512]{0:T(512)S(1)} %broadcast_multiply_fusion.1) | copy-start | bytes 6148
  10.9 51.3 %copy-start.42 = (f32[512]{0:T(512)}, f32[512]{0:T(512)S(1)}, u32[]{:S(2)}) copy-start(f32[512]{0:T(512)S(1)} %fusion.109) | copy-start | bytes 6148
  11.0 51.3 %copy-start.40 = (f32[512]{0:T(512)}, f32[512]{0:T(512)S(1)}, u32[]{:S(2)}) copy-start(f32[512]{0:T(512)S(1)} %fusion.122) | copy-start | bytes 6148
  62.2 268.6 %reduce-scatter.19.cloned.1.call-start = ((), (), s32[]{:S(2)}) async-start(), calls=%async_computation.11 | async-start | bytes 3932160 | tf_op jit(solution)/shard_map/reduce_scatter | solution.py:158
  93.5 198.3 %copy-start.13 = (bf16[192,768]{0,1:T(8,128)(2,1)}, bf16[192,768]{0,1:T(8,128)(2,1)S(1)}, u32[]{:S(2)}) copy-start(bf16[192,768]{0,1:T(8,128)(2,1)S(1)} %all_gather.71) | copy-start | bytes 884740
  124.5 62.1 %copy-start.26 = (bf16[768,192]{1,0:T(8,128)(2,1)}, bf16[768,192]{1,0:T(8,128)(2,1)S(1)}, u32[]{:S(2)}) copy-start(bf16[768,192]{1,0:T(8,128)(2,1)S(1)} %all_gather.66) | copy-start | bytes 884740
  155.5 31.1 %copy-start.28 = (bf16[768,192]{1,0:T(8,128)(2,1)}, bf16[768,192]{1,0:T(8,128)(2,1)S(1)}, u32[]{:S(2)}) copy-start(bf16[768,192]{1,0:T(8,128)(2,1)S(1)} %all_gather.67) | copy-start | bytes 884740
  292.7 38.1 %copy-start.1 = (bf16[512,768]{1,0:T(8,128)(2,1)S(1)}, bf16[512,768]{1,0:T(8,128)(2,1)}, u32[]{:S(2)}) copy-start(bf16[512,768]{1,0:T(8,128)(2,1)} %param.22) | copy-start | bytes 2359300
  295.4 67.8 %all-gather.12.cloned.1.call-start = ((), (), s32[]{:S(2)}) async-start(), calls=%async_computation.13 | async-start | bytes 1327104 | tf_op jit(solution)/shard_map/all_gather | solution.py:88
  296.0 70.1 %all-gather.10.cloned.1.call-start = ((), (), s32[]{:S(2)}) async-start(), calls=%async_computation.12 | async-start | bytes 3932160 | tf_op jit(solution)/shard_map/all_gather | solution.py:163
  335.3 74.6 %all-gather.14.cloned.1.call-start = ((), (), s32[]{:S(2)}) async-start(), calls=%async_computation.14 | async-start | bytes 1327104 | tf_op jit(solution)/shard_map/all_gather | solution.py:90
  335.9 102.6 %all-gather.16.cloned.1.call-start = ((), (), s32[]{:S(2)}) async-start(), calls=%async_computation.16 | async-start | bytes 3932160 | tf_op jit(solution)/shard_map/all_gather | solution.py:183
  336.7 166.2 %reduce-scatter.23.cloned.1.call-start = ((), (), s32[]{:S(2)}) async-start(), calls=%async_computation.17 | async-start | bytes 3932160 | tf_op jit(solution)/shard_map/reduce_scatter | solution.py:191
  438.5 22.3 %copy-start.49 = (bf16[768,768]{1,0:T(8,128)(2,1)S(1)}, bf16[768,768]{1,0:T(8,128)(2,1)}, u32[]{:S(2)}) copy-start(bf16[768,768]{1,0:T(8,128)(2,1)} %all-gather.12.cloned.1.call-done) | copy-start | bytes 3538948
  464.8 78.5 %reduce-scatter.21.cloned.1.call-start = ((), (), s32[]{:S(2)}) async-start(), calls=%async_computation.15 | async-start | bytes 3932160 | tf_op jit(solution)/shard_map/reduce_scatter | solution.py:167
  464.8 7.2 copy-start.50
  476.1 101.8 %all-gather.18.cloned.1.call-start = ((), (), s32[]{:S(2)}) async-start(), calls=%async_computation.18 | async-start | bytes 3932160 | tf_op jit(solution)/shard_map/all_gather | solution.py:202
  547.3 30.7 %copy-start.18 = (bf16[4,24,8,512]{3,2,0,1:T(8,128)(2,1)S(1)}, bf16[4,24,8,512]{3,2,0,1:T(8,128)(2,1)}, u32[]{:S(2)}) copy-start(bf16[4,24,8,512]{3,2,0,1:T(8,128)(2,1)} %copy-done.17) | copy-start | bytes 2359300
  549.4 336.2 %reduce-scatter.37.cloned.1.call-start = ((), (), s32[]{:S(2)}) async-start(), calls=%async_computation.25 | async-start | bytes 884736
  549.5 32.6 %copy-start.14 = (bf16[192,768]{0,1:T(8,128)(2,1)S(1)}, bf16[192,768]{0,1:T(8,128)(2,1)}, u32[]{:S(2)}) copy-start(bf16[192,768]{0,1:T(8,128)(2,1)} %copy-done.13) | copy-start | bytes 884740
  582.1 6.8 copy-start.11
  582.1 314.7 %reduce-scatter.25.cloned.1.call-start = ((), (), s32[]{:S(2)}) async-start(), calls=%async_computation.19 | async-start | bytes 3932160 | tf_op jit(solution)/shard_map/reduce_scatter | solution.py:251
  596.7 7.2 copy-start
  661.5 7.2 copy-start
  725.8 7.2 copy-start
  790.1 7.2 copy-start
  858.8 111.9 %reduce-scatter.29.cloned.1.call-start = ((), (), s32[]{:S(2)}) async-start(), calls=%async_computation.21 | async-start | bytes 2654208 | tf_op jit(solution)/shard_map/reduce_scatter | solution.py:299
  866.7 7.7 copy-start.21
  866.7 7.7 copy-start.23
  866.7 7.7 copy-start.25
  866.7 176.5 %reduce-scatter.27.cloned.1.call-start = ((), (), s32[]{:S(2)}) async-start(), calls=%async_computation.20 | async-start | bytes 2654208 | tf_op jit(solution)/shard_map/reduce_scatter | solution.py:298
  874.3 234.8 %reduce-scatter.35.cloned.1.call-start = ((), (), s32[]{:S(2)}) async-start(), calls=%async_computation.24 | async-start | bytes 884736
  879.6 294.9 %reduce-scatter.33.cloned.1.call-start = ((), (), s32[]{:S(2)}) async-start(), calls=%async_computation.23 | async-start | bytes 884736
  879.7 18.4 %copy-start.2 = (bf16[512,768]{1,0:T(8,128)(2,1)S(1)}, bf16[512,768]{1,0:T(8,128)(2,1)}, u32[]{:S(2)}) copy-start(bf16[512,768]{1,0:T(8,128)(2,1)} %param.22) | copy-start | bytes 2359300
  879.7 18.4 %copy-start.33 = (f32[768]{0:T(1024)S(1)}, f32[768]{0:T(1024)}, u32[]{:S(2)}) copy-start(f32[768]{0:T(1024)} %copy-done.32) | copy-start | bytes 9220
  879.7 18.4 %copy-start.35 = (f32[512]{0:T(512)S(1)}, f32[512]{0:T(512)}, u32[]{:S(2)}) copy-start(f32[512]{0:T(512)} %copy-done.34) | copy-start | bytes 6148
  880.9 359.5 %reduce-scatter.31.cloned.1.call-start = ((), (), s32[]{:S(2)}) async-start(), calls=%async_computation.22 | async-start | bytes 884736
  882.3 17.4 %copy-start.43 = (f32[512]{0:T(512)S(1)}, f32[512]{0:T(512)}, u32[]{:S(2)}) copy-start(f32[512]{0:T(512)} %copy-done.42) | copy-start | bytes 6148
  882.3 17.4 %copy-start.41 = (f32[512]{0:T(512)S(1)}, f32[512]{0:T(512)}, u32[]{:S(2)}) copy-start(f32[512]{0:T(512)} %copy-done.40) | copy-start | bytes 6148
  884.0 17.8 %copy-start.44 = (bf16[768]{0:T(1024)(128)(2,1)S(1)}, bf16[768]{0:T(1024)(128)(2,1)}, u32[]{:S(2)}) copy-start(bf16[768]{0:T(1024)(128)(2,1)} %get-tuple-element.387) | copy-start | bytes 4612
  884.0 17.9 %copy-start.45 = (bf16[768]{0:T(1024)(128)(2,1)S(1)}, bf16[768]{0:T(1024)(128)(2,1)}, u32[]{:S(2)}) copy-start(bf16[768]{0:T(1024)(128)(2,1)} %get-tuple-element.316) | copy-start | bytes 4612
  884.0 72.3 %copy-start.5 = (f32[512,768]{1,0:T(8,128)S(1)}, f32[512,768]{1,0:T(8,128)}, u32[]{:S(2)}) copy-start(f32[512,768]{1,0:T(8,128)} %copy-done.4) | copy-start | bytes 4718596
  896.7 59.5 %copy-start.7 = (bf16[512,768]{1,0:T(8,128)(2,1)S(1)}, bf16[512,768]{1,0:T(8,128)(2,1)}, u32[]{:S(2)}) copy-start(bf16[512,768]{1,0:T(8,128)(2,1)} %reduce-scatter.25.cloned.1.call-done) | copy-start | bytes 2359300
  (26 other events, 66.4 us)
Sparse Core Ops, SparseCore 0:
  62.3 25.7 all-gather.7
  295.5 35.2 reduce-scatter.18
  464.9 37.9 reduce-scatter.22
  505.2 37.9 reduce-scatter.20
Sparse Core Ops, SparseCore 1:
  298.3 38.8 all-gather.11
  339.2 26.8 all-gather.9
  368.4 41.5 all-gather.13
  411.6 26.8 all-gather.15
  549.5 28.3 all-gather.17
  582.1 62.5 reduce-scatter.36
  858.9 37.8 reduce-scatter.24
  901.1 69.5 reduce-scatter.28
  975.0 68.2 reduce-scatter.26
  1047.5 61.6 reduce-scatter.34
  1112.9 61.6 reduce-scatter.32
  1178.8 61.6 reduce-scatter.30
where the time goes:
time: 1250 us
  waiting for transfers between devices  487 us (39%)
  matrix products  358 us (29%)
  blocking collectives  239 us (19%)
  other arithmetic  70.1 us (6%)
  local copies, waits for them, and re-layouts  42.9 us (3%)
  loops' own time  31.9 us (3%)
  between operations  18.4 us (1%)
    unnamed x20, waiting for transfers between devices  199 us
    dot_general x4, matrix products, backward_block(): jnp.einsum('hqk,qhd->khd', grad_raw, query_block, preferred_element_type=...  89.7 us
    dot_general x4, matrix products, backward_block(): jnp.einsum('hqk,khd->qhd', grad_raw, key_seq, preferred_element_type=f32)  83.1 us
    unnamed x2, blocking collectives  78.3 us
    reduce_scatter x1, waiting for transfers between devices, per_device(): lax.psum_scatter(grad_w_in, 'dp', scatter_dimension=0, tiled=True)  72.6 us
    all_gather x1, waiting for transfers between devices, per_device(): lax.all_gather(w_back, 'dp', axis=1, tiled=True)  36.3 us
    reduce_scatter x1, waiting for transfers between devices, per_device(): lax.psum_scatter(mlp_part, 'tensor', scatter_dimension=0, tiled=True)  35.9 us
    reduce_scatter x1, waiting for transfers between devices, per_device(): lax.psum_scatter(attn_part, 'tensor', scatter_dimension=0, tiled=True)  34.7 us
  transfers between devices with their start and end apart: 16, of which 13 were waited for; matrix products, arithmetic and copies ran while one was open for 26% of the time, Pallas kernels for 0%

commit v1 on v0

--- a/solution.py
+++ b/solution.py
@@ -6,6 +6,12 @@
 
 HEAD_DIM = 64
 EPSILON = 1e-12
+
+
+def divide_row(m, where_dim):
+    block_out = list(m.shape[1:])
+    block_out[where_dim] *= m.shape[0]
+    return jnp.moveaxis(m, 0, where_dim).reshape(block_out)
 
 
 def layer_norm(values, gain, shift):
@@ -57,6 +63,17 @@
     f32 = jnp.float32
     bf16 = jnp.bfloat16
     index = lax.axis_index("tensor")
+
+    def note_circles_all(local_values, mesh_dim, k_dim):
+        fan = lax.axis_size(mesh_dim)
+        pool = list(map(lambda ii: (ii, (ii + 1) % fan), range(fan)))
+        tray = [local_values]
+        while len(tray) < fan:
+            tray.append(lax.ppermute(tray[-1], mesh_dim, pool))
+        known = lax.axis_index(mesh_dim)
+        tray = jnp.stack(tray)[(known - jnp.arange(fan)) % fan]
+        return divide_row(tray, k_dim)
+
     (
         gain_one,
         shift_one,
@@ -78,7 +95,7 @@
         lax.all_gather(ln1_bias, "dp", axis=0, tiled=True),
         lax.all_gather(w_query, "dp", axis=0, tiled=True),
         lax.all_gather(query_bias, "dp", axis=0, tiled=True),
-        lax.all_gather(w_key, "dp", axis=0, tiled=True),
+        note_circles_all(w_key, "dp", 0),
         lax.all_gather(w_value, "dp", axis=0, tiled=True),
         lax.all_gather(value_bias, "dp", axis=0, tiled=True),
         lax.all_gather(w_out, "dp", axis=1, tiled=True),

time: 1250 us -> 1270 us (1.016)
    ppermute x0 -> x7, waiting for transfers between devices: none -> 38.8 us  [note_circles_all(): tray.append(lax.ppermute(tray[-1], mesh_dim, pool))]
    all_gather x1, waiting for transfers between devices: 28.4 us -> 0.01 us  [per_device(): middle_rows = lax.all_gather(middle_low, 'tensor', axis=0, tiled=True)]
    unnamed x134 -> x127, local copies, waits for them, and re-layouts: 28.6 us -> 25.2 us
  transfers between devices with their start and end apart: 16 -> 23, of which waited for: 13 -> 18; matrix products, arithmetic and copies ran while one was open for 26% -> 25% of each run, Pallas kernels for 0% -> 0%
where the time goes in v1:
time: 1270 us; the launch traced here: 1260 us
  waiting for transfers between devices  498 us (39%)
  matrix products  359 us (28%)
  blocking collectives  241 us (19%)
  other arithmetic  69.6 us (5%)
  local copies, waits for them, and re-layouts  40.1 us (3%)
  loops' own time  31.9 us (3%)
  between operations  18.5 us (1%)
    unnamed x20, waiting for transfers between devices  199 us
    dot_general x4, matrix products, backward_block(): jnp.einsum('hqk,qhd->khd', grad_raw, query_block, preferred_element_type=...  89.7 us
    dot_general x4, matrix products, backward_block(): jnp.einsum('hqk,khd->qhd', grad_raw, key_seq, preferred_element_type=f32)  83.1 us
    unnamed x2, blocking collectives  77.6 us
    reduce_scatter x1, waiting for transfers between devices, per_device(): lax.psum_scatter(grad_w_in, 'dp', scatter_dimension=0, tiled=True)  72.3 us
    ppermute x7, waiting for transfers between devices, note_circles_all(): tray.append(lax.ppermute(tray[-1], mesh_dim, pool))  38.8 us
    all_gather x1, waiting for transfers between devices, per_device(): lax.all_gather(w_back, 'dp', axis=1, tiled=True)  36.3 us
    reduce_scatter x1, waiting for transfers between devices, per_device(): lax.psum_scatter(mlp_part, 'tensor', scatter_dimension=0, tiled=True)  35.9 us
  transfers between devices with their start and end apart: 23, of which 18 were waited for; matrix products, arithmetic and copies ran while one was open for 25% of the time, Pallas kernels for 0%

profile of v1, /device:TPU:0, one launch (start us, length us, event | category | flops | bytes accessed | tf_op | source)
XLA Modules:
  0.0 1260.6 jit_solution(5303639133420362494)
XLA Ops:
  19.7 39.4 %all-reduce.18 = (bf16[768]{0:T(1024)(128)(2,1)S(1)}, bf16[768]{0:T(1024)(128)(2,1)S(1)}, bf16[768]{0:T(1024)(128)(2,1)S(1)}, bf16[768]{0:T(1024)(128)(2,1)S(1)}...) all-reduce(bf16[768]{0:T(1024)(128)(2,1)S(1)} %dynamic-update-slice, ...), channel_id=1, replica_groups=mesh['dp'=8,'tensor'=4] {'dp'}, use_global_device_ids=true, to_apply=%add.1 | all-reduce | flops 6144 | bytes 24576
  61.8 31.0 %all_gather.69 = bf16[192,768]{0,1:T(8,128)(2,1)S(1)} all-gather(bf16[192,96]{0,1:T(8,128)(2,1)S(1)} %copy.44), channel_id=1, replica_groups=mesh['dp'=8,'tensor'=4] {'dp'}, dimensions={1}, use_global_device_ids=true | all-gather | bytes 331776 | tf_op jit(solution)/shard_map/all_gather | solution.py:101
  92.8 31.4 %all_gather.65 = bf16[768,192]{1,0:T(8,128)(2,1)S(1)} all-gather(bf16[96,192]{1,0:T(8,128)(2,1)S(1)} %copy-done.30), channel_id=1, replica_groups=mesh['dp'=8,'tensor'=4] {'dp'}, dimensions={0}, use_global_device_ids=true | all-gather | bytes 331776 | tf_op jit(solution)/shard_map/all_gather | solution.py:96
  124.2 31.0 %all_gather.66 = bf16[768,192]{1,0:T(8,128)(2,1)S(1)} all-gather(bf16[96,192]{1,0:T(8,128)(2,1)S(1)} %copy-done.31), channel_id=1, replica_groups=mesh['dp'=8,'tensor'=4] {'dp'}, dimensions={0}, use_global_device_ids=true | all-gather | bytes 331776 | tf_op jit(solution)/shard_map/all_gather | solution.py:99
  162.1 6.8 collective-permute-done.2
  168.9 6.8 collective-permute-done.3
  175.6 6.8 collective-permute-done.4
  182.4 6.8 collective-permute-done.5
  189.4 6.8 collective-permute-done.6
  201.6 98.7 %while.30 = (s32[]{:T(128)}, bf16[4,512,192]{1,2,0:T(8,128)(2,1)}, f32[4,3,512]{2,1,0:T(4,128)S(1)}, s32[4]{0:T(128)S(1)}, s32[1,2048]{1,0:T(1,128)S(1)}, /*inde...) while((s32[]{:T(128)}, bf16[4,512,192]{1,2,0:T(8,128)(2,1)}, ...), condition=%wide.region_5.6_spmd, body=%wide.region_2.5_spmd.sunk | while | flops 844200448 | bytes 44372400 | solution.py:172
  212.1 6.8 fusion.182
  218.9 6.7 fusion.183
  236.8 6.8 fusion.182
  261.5 6.8 fusion.182
  268.3 6.7 fusion.183
  286.2 6.8 fusion.182
  306.1 34.5 %reduce-scatter.19.cloned.1.call-done = bf16[512,768]{1,0:T(8,128)(2,1)} async-done(((bf16[2048,768]{1,0:T(8,128)(2,1)}), bf16[512,768]{1,0:T(8,128)(2,1)}) %reduce-scatter.19.cloned.1.call-update) | async-done | bytes 786448 | tf_op jit(solution)/shard_map/reduce_scatter | solution.py:175
  346.5 26.5 %all-gather = bf16[8,1,384]{2,1,0:T(2,128)(2,1)S(1)} all-gather(bf16[1,1,384]{2,1,0:T(2,128)(2,1)S(1)} %reshape.343), channel_id=1, replica_groups=mesh['dp'=8,'tensor'=4] {'dp'}, dimensions={0}, use_global_device_ids=true | all-gather | bytes 6912 | tf_op jit(solution)/shard_map/all_gather | solution.py:106
  375.9 7.6 fusion.139
  383.5 36.3 %all-gather.14.cloned.1.call-done = bf16[768,768]{0,1:T(8,128)(2,1)} async-done(((bf16[768,96]{0,1:T(8,128)(2,1)}), bf16[768,768]{0,1:T(8,128)(2,1)}) %all-gather.14.cloned.1.call-update) | async-done | bytes 1179664 | tf_op jit(solution)/shard_map/all_gather | solution.py:107
  419.8 28.5 %all-gather.16.cloned.1.call-done = bf16[2048,768]{1,0:T(8,128)(2,1)} async-done(((bf16[512,768]{1,0:T(8,128)(2,1)}), bf16[2048,768]{1,0:T(8,128)(2,1)}) %all-gather.16.cloned.1.call-update) | async-done | bytes 3145744 | tf_op jit(solution)/shard_map/all_gather | solution.py:200
  448.3 20.5 %fusion.132 = (bf16[768]{0:T(1024)(128)(2,1)}, bf16[2048,768]{1,0:T(8,128)(2,1)S(1)}, f32[2048,768]{1,0:T(8,128)}) fusion(f32[2048,768]{1,0:T(8,128)} %fusion.139, f32[768]{0:T(1024)S(1)} %dynamic-slice_convert_fusion, bf16[2048,768]{1,0:T(8,128)(2,1)} %all-gather.16.cloned.1.call-done, bf16[768,768]{0,1:T(8,128)(2,1)} %all-gather.14.cloned.1.call-done), kind=kOutput, calls=%fused_computation.174 | convolution fusion | flops 2532310272 | bytes 20058624 | tf_op jit(solution)/shard_map/dot_general | solution.py:34
  486.5 26.1 %reduce-scatter.23.cloned.1.call-done = bf16[512,768]{1,0:T(8,128)(2,1)} async-done(((bf16[2048,768]{1,0:T(8,128)(2,1)}), bf16[512,768]{1,0:T(8,128)(2,1)}) %reduce-scatter.23.cloned.1.call-update) | async-done | bytes 786448 | tf_op jit(solution)/shard_map/reduce_scatter | solution.py:208
  517.1 35.9 %reduce-scatter.21.cloned.1.call-done = bf16[512,768]{1,0:T(8,128)(2,1)} async-done(((bf16[2048,768]{1,0:T(8,128)(2,1)}), bf16[512,768]{1,0:T(8,128)(2,1)}) %reduce-scatter.21.cloned.1.call-update) | async-done | bytes 786448 | tf_op jit(solution)/shard_map/reduce_scatter | solution.py:184
  559.2 33.1 %all_gather.80 = bf16[768,192]{1,0:T(8,128)(2,1)} all-gather(bf16[96,192]{1,0:T(8,128)(2,1)S(1)} %copy-done.25), channel_id=1, replica_groups=mesh['dp'=8,'tensor'=4] {'dp'}, dimensions={0}, use_global_device_ids=true | all-gather | bytes 331776 | tf_op jit(solution)/shard_map/all_gather | solution.py:191
  603.3 258.0 %while.31 = (s32[]{:T(128)}, f32[1,2048,3,64]{1,3,2,0:T(8,128)}, f32[1,2048,3,64]{1,3,2,0:T(8,128)}, f32[4,512,3,64]{1,3,2,0:T(8,128)}, s32[4]{0:T(128)S(1)}, /*...) while((s32[]{:T(128)}, f32[1,2048,3,64]{1,3,2,0:T(8,128)}, ...), condition=%wide.region_15.16_spmd, body=%wide.region_13.15_spmd.sunk | while | flops 2096897024 | bytes 208079408 | solution.py:255
  611.2 7.2 fusion.197
  624.7 20.9 %fusion.198 = f32[4,512,3,64]{1,3,2,0:T(8,128)} fusion(f32[4,512,3,64]{1,3,2,0:T(8,128)} %get-tuple-element.595, s32[]{:T(128)S(6)} %copy.90, f32[3,512,2048]{2,1,0:T(8,128)} %fusion.194, f32[3,512,2048]{2,1,0:T(8,128)} %copy-done, f32[3,512]{1,0:T(4,128)S(1)} %dynamic-slice_bitcast_fusion.2, pred[512,2048]{1,0:T(8,128)(4,1)S(1)} %broadcast_compare_fusion.5, ...), kind=kOutput, calls=%fused_computation.45.clone.1 | convolution fusion | flops 437259776 | bytes 53624836 | tf_op jit(solution)/shard_map/while/body/eval_jaxpr/hqk,khd->qhd/dot_general | solution.py:237
  645.7 22.6 %fusion.196 = f32[1,2048,3,64]{1,3,2,0:T(8,128)} fusion(f32[3,512,2048]{2,1,0:T(8,128)} %fusion.194, f32[3,512,2048]{2,1,0:T(8,128)} %copy-done, f32[3,512]{1,0:T(4,128)S(1)} %dynamic-slice_bitcast_fusion.2, pred[512,2048]{1,0:T(8,128)(4,1)S(1)} %broadcast_compare_fusion.5, f32[1,2048,3,64]{1,3,2,0:T(8,128)} %get-tuple-element.593, ...), kind=kOutput, calls=%fused_computation.40.clone.1 | convolution fusion | flops 437652992 | bytes 55787524 | tf_op jit(solution)/shard_map/while/body/eval_jaxpr/hqk,qhd->khd/dot_general | solution.py:238
  675.9 7.2 fusion.197
  689.4 20.7 %fusion.198 = f32[4,512,3,64]{1,3,2,0:T(8,128)} fusion(f32[4,512,3,64]{1,3,2,0:T(8,128)} %get-tuple-element.595, s32[]{:T(128)S(6)} %copy.90, f32[3,512,2048]{2,1,0:T(8,128)} %fusion.194, f32[3,512,2048]{2,1,0:T(8,128)} %copy-done, f32[3,512]{1,0:T(4,128)S(1)} %dynamic-slice_bitcast_fusion.2, pred[512,2048]{1,0:T(8,128)(4,1)S(1)} %broadcast_compare_fusion.5, ...), kind=kOutput, calls=%fused_computation.45.clone.1 | convolution fusion | flops 437259776 | bytes 53624836 | tf_op jit(solution)/shard_map/while/body/eval_jaxpr/hqk,khd->qhd/dot_general | solution.py:237
  710.2 22.4 %fusion.196 = f32[1,2048,3,64]{1,3,2,0:T(8,128)} fusion(f32[3,512,2048]{2,1,0:T(8,128)} %fusion.194, f32[3,512,2048]{2,1,0:T(8,128)} %copy-done, f32[3,512]{1,0:T(4,128)S(1)} %dynamic-slice_bitcast_fusion.2, pred[512,2048]{1,0:T(8,128)(4,1)S(1)} %broadcast_compare_fusion.5, f32[1,2048,3,64]{1,3,2,0:T(8,128)} %get-tuple-element.593, ...), kind=kOutput, calls=%fused_computation.40.clone.1 | convolution fusion | flops 437652992 | bytes 55787524 | tf_op jit(solution)/shard_map/while/body/eval_jaxpr/hqk,qhd->khd/dot_general | solution.py:238
  740.2 7.2 fusion.197
  753.7 20.7 %fusion.198 = f32[4,512,3,64]{1,3,2,0:T(8,128)} fusion(f32[4,512,3,64]{1,3,2,0:T(8,128)} %get-tuple-element.595, s32[]{:T(128)S(6)} %copy.90, f32[3,512,2048]{2,1,0:T(8,128)} %fusion.194, f32[3,512,2048]{2,1,0:T(8,128)} %copy-done, f32[3,512]{1,0:T(4,128)S(1)} %dynamic-slice_bitcast_fusion.2, pred[512,2048]{1,0:T(8,128)(4,1)S(1)} %broadcast_compare_fusion.5, ...), kind=kOutput, calls=%fused_computation.45.clone.1 | convolution fusion | flops 437259776 | bytes 53624836 | tf_op jit(solution)/shard_map/while/body/eval_jaxpr/hqk,khd->qhd/dot_general | solution.py:237
  774.5 22.4 %fusion.196 = f32[1,2048,3,64]{1,3,2,0:T(8,128)} fusion(f32[3,512,2048]{2,1,0:T(8,128)} %fusion.194, f32[3,512,2048]{2,1,0:T(8,128)} %copy-done, f32[3,512]{1,0:T(4,128)S(1)} %dynamic-slice_bitcast_fusion.2, pred[512,2048]{1,0:T(8,128)(4,1)S(1)} %broadcast_compare_fusion.5, f32[1,2048,3,64]{1,3,2,0:T(8,128)} %get-tuple-element.593, ...), kind=kOutput, calls=%fused_computation.40.clone.1 | convolution fusion | flops 437652992 | bytes 55787524 | tf_op jit(solution)/shard_map/while/body/eval_jaxpr/hqk,qhd->khd/dot_general | solution.py:238
  804.5 7.2 fusion.197
  818.0 20.8 %fusion.198 = f32[4,512,3,64]{1,3,2,0:T(8,128)} fusion(f32[4,512,3,64]{1,3,2,0:T(8,128)} %get-tuple-element.595, s32[]{:T(128)S(6)} %copy.90, f32[3,512,2048]{2,1,0:T(8,128)} %fusion.194, f32[3,512,2048]{2,1,0:T(8,128)} %copy-done, f32[3,512]{1,0:T(4,128)S(1)} %dynamic-slice_bitcast_fusion.2, pred[512,2048]{1,0:T(8,128)(4,1)S(1)} %broadcast_compare_fusion.5, ...), kind=kOutput, calls=%fused_computation.45.clone.1 | convolution fusion | flops 437259776 | bytes 53624836 | tf_op jit(solution)/shard_map/while/body/eval_jaxpr/hqk,khd->qhd/dot_general | solution.py:237
  838.8 22.4 %fusion.196 = f32[1,2048,3,64]{1,3,2,0:T(8,128)} fusion(f32[3,512,2048]{2,1,0:T(8,128)} %fusion.194, f32[3,512,2048]{2,1,0:T(8,128)} %copy-done, f32[3,512]{1,0:T(4,128)S(1)} %dynamic-slice_bitcast_fusion.2, pred[512,2048]{1,0:T(8,128)(4,1)S(1)} %broadcast_compare_fusion.5, f32[1,2048,3,64]{1,3,2,0:T(8,128)} %get-tuple-element.593, ...), kind=kOutput, calls=%fused_computation.40.clone.1 | convolution fusion | flops 437652992 | bytes 55787524 | tf_op jit(solution)/shard_map/while/body/eval_jaxpr/hqk,qhd->khd/dot_general | solution.py:238
  871.8 7.0 fusion.140
  878.9 7.6 fusion.114
  899.5 10.3 reduce-scatter.25.cloned.1.call-done
  914.9 10.3 all-reduce.19
  925.1 38.2 %all-reduce.17 = (f32[768]{0:T(1024)S(1)}, f32[768]{0:T(1024)S(1)}, f32[768]{0:T(1024)S(1)}, f32[768]{0:T(1024)S(1)}, f32[768]{0:T(1024)S(1)}, /*index=5*/f32[76...) all-reduce(bf16[768]{0:T(1024)(128)(2,1)S(1)} %get-tuple-element.37, ...), channel_id=6, replica_groups=mesh['dp'=8,'tensor'=4] {'dp'}, use_global_device_ids=true, to_apply=%region_21.22.clone | all-reduce | flops 9216 | bytes 55296
  970.3 13.2 %reduce-scatter.29.cloned.1.call-done = f32[768,96]{0,1:T(8,128)} async-done(((f32[768,768]{0,1:T(8,128)}), f32[768,96]{0,1:T(8,128)}) %reduce-scatter.29.cloned.1.call-update) | async-done | bytes 294928 | tf_op jit(solution)/shard_map/reduce_scatter | solution.py:316
  983.6 72.3 %reduce-scatter.27.cloned.1.call-done = f32[96,768]{1,0:T(8,128)} async-done(((f32[768,768]{1,0:T(8,128)}), f32[96,768]{1,0:T(8,128)}) %reduce-scatter.27.cloned.1.call-update) | async-done | bytes 294928 | tf_op jit(solution)/shard_map/reduce_scatter | solution.py:315
  1055.9 65.9 %reduce-scatter.35.cloned.1.call-done = f32[96,192]{1,0:T(8,128)} async-done(((f32[768,192]{1,0:T(8,128)}), f32[96,192]{1,0:T(8,128)}) %reduce-scatter.35.cloned.1.call-update) | async-done | bytes 73744
  1121.7 65.4 %reduce-scatter.33.cloned.1.call-done = f32[96,192]{1,0:T(8,128)} async-done(((f32[768,192]{1,0:T(8,128)}), f32[96,192]{1,0:T(8,128)}) %reduce-scatter.33.cloned.1.call-update) | async-done | bytes 73744
  1187.1 65.9 %reduce-scatter.31.cloned.1.call-done = f32[96,192]{1,0:T(8,128)} async-done(((f32[768,192]{1,0:T(8,128)}), f32[96,192]{1,0:T(8,128)}) %reduce-scatter.31.cloned.1.call-update) | async-done | bytes 73744
  (308 shorter events, 196.6 us)
Async XLA Ops:
  8.0 53.5 %copy-start.24 = (bf16[96,192]{1,0:T(8,128)(2,1)S(1)}, bf16[96,192]{1,0:T(8,128)(2,1)}, u32[]{:S(2)}) copy-start(bf16[96,192]{1,0:T(8,128)(2,1)} %param.29) | copy-start | bytes 110596
  8.0 53.6 %copy-start.32 = (bf16[192,96]{1,0:T(8,128)(2,1)S(1)}, bf16[192,96]{1,0:T(8,128)(2,1)}, u32[]{:S(2)}) copy-start(bf16[192,96]{1,0:T(8,128)(2,1)} %param.32) | copy-start | bytes 110596
  8.0 84.7 %copy-start.30 = (bf16[96,192]{1,0:T(8,128)(2,1)S(1)}, bf16[96,192]{1,0:T(8,128)(2,1)}, u32[]{:S(2)}) copy-start(bf16[96,192]{1,0:T(8,128)(2,1)} %param.27) | copy-start | bytes 110596
  8.1 116.1 %copy-start.31 = (bf16[96,192]{1,0:T(8,128)(2,1)S(1)}, bf16[96,192]{1,0:T(8,128)(2,1)}, u32[]{:S(2)}) copy-start(bf16[96,192]{1,0:T(8,128)(2,1)} %param.30) | copy-start | bytes 110596
  8.1 188.7 %all-gather.8.cloned.1.call-start = ((), (), s32[]{:S(2)}) async-start(), calls=%async_computation.10 | async-start | bytes 3932160 | tf_op jit(solution)/shard_map/all_gather | solution.py:125
  9.4 52.2 %copy-start.28 = (f32[512]{0:T(512)}, f32[512]{0:T(512)S(1)}, u32[]{:S(2)}) copy-start(f32[512]{0:T(512)S(1)} %broadcast_multiply_fusion.1) | copy-start | bytes 6148
  10.9 48.2 %copy-start.35 = (f32[512]{0:T(512)}, f32[512]{0:T(512)S(1)}, u32[]{:S(2)}) copy-start(f32[512]{0:T(512)S(1)} %fusion.109) | copy-start | bytes 6148
  11.0 50.7 %copy-start.33 = (f32[512]{0:T(512)}, f32[512]{0:T(512)S(1)}, u32[]{:S(2)}) copy-start(f32[512]{0:T(512)S(1)} %fusion.124) | copy-start | bytes 6148
  59.1 65.1 %copy-start.26 = (f32[768]{0:T(1024)}, f32[768]{0:T(1024)S(1)}, u32[]{:S(2)}) copy-start(f32[768]{0:T(1024)S(1)} %convert_element_type.172) | copy-start | bytes 9220
  61.5 279.1 %reduce-scatter.19.cloned.1.call-start = ((), (), s32[]{:S(2)}) async-start(), calls=%async_computation.11 | async-start | bytes 3932160 | tf_op jit(solution)/shard_map/reduce_scatter | solution.py:175
  61.6 93.7 %collective-permute-start = (bf16[96,192]{1,0:T(8,128)(2,1)S(1)}, bf16[96,192]{1,0:T(8,128)(2,1)S(1)}, u32[]{:S(2)}, u32[]{:S(2)}) collective-permute-start(bf16[96,192]{1,0:T(8,128)(2,1)S(1)} %copy-done.24), channel_id=1, source_target_pairs={{0,4},{4,8},{8,12},{12,16},{16,20},{20,24},{24,28},{28,0},{1,5},{5... | collective-permute-start | bytes 110600 | tf_op jit(solution)/shard_map/ppermute | solution.py:72
  92.8 209.1 %copy-start.13 = (bf16[192,768]{0,1:T(8,128)(2,1)}, bf16[192,768]{0,1:T(8,128)(2,1)S(1)}, u32[]{:S(2)}) copy-start(bf16[192,768]{0,1:T(8,128)(2,1)S(1)} %all_gather.69) | copy-start | bytes 884740
  124.2 72.6 %copy-start.19 = (bf16[768,192]{1,0:T(8,128)(2,1)}, bf16[768,192]{1,0:T(8,128)(2,1)S(1)}, u32[]{:S(2)}) copy-start(bf16[768,192]{1,0:T(8,128)(2,1)S(1)} %all_gather.65) | copy-start | bytes 884740
  155.2 45.7 %copy-start.21 = (bf16[768,192]{1,0:T(8,128)(2,1)}, bf16[768,192]{1,0:T(8,128)(2,1)S(1)}, u32[]{:S(2)}) copy-start(bf16[768,192]{1,0:T(8,128)(2,1)S(1)} %all_gather.66) | copy-start | bytes 884740
  155.2 6.8 collective-permute-start.1
  162.1 6.8 collective-permute-start.2
  168.8 6.8 collective-permute-start.3
  175.6 6.8 collective-permute-start.4
  182.4 6.8 collective-permute-start.5
  189.2 7.0 collective-permute-start.6
  302.8 37.9 %copy-start.1 = (bf16[512,768]{1,0:T(8,128)(2,1)S(1)}, bf16[512,768]{1,0:T(8,128)(2,1)}, u32[]{:S(2)}) copy-start(bf16[512,768]{1,0:T(8,128)(2,1)} %param.22) | copy-start | bytes 2359300
  305.5 67.7 %all-gather.12.cloned.1.call-start = ((), (), s32[]{:S(2)}) async-start(), calls=%async_computation.13 | async-start | bytes 1327104 | tf_op jit(solution)/shard_map/all_gather | solution.py:105
  306.0 69.9 %all-gather.10.cloned.1.call-start = ((), (), s32[]{:S(2)}) async-start(), calls=%async_computation.12 | async-start | bytes 3932160 | tf_op jit(solution)/shard_map/all_gather | solution.py:180
  345.1 74.6 %all-gather.14.cloned.1.call-start = ((), (), s32[]{:S(2)}) async-start(), calls=%async_computation.14 | async-start | bytes 1327104 | tf_op jit(solution)/shard_map/all_gather | solution.py:107
  345.7 102.6 %all-gather.16.cloned.1.call-start = ((), (), s32[]{:S(2)}) async-start(), calls=%async_computation.16 | async-start | bytes 3932160 | tf_op jit(solution)/shard_map/all_gather | solution.py:200
  346.5 166.1 %reduce-scatter.23.cloned.1.call-start = ((), (), s32[]{:S(2)}) async-start(), calls=%async_computation.17 | async-start | bytes 3932160 | tf_op jit(solution)/shard_map/reduce_scatter | solution.py:208
  448.3 22.2 %copy-start.42 = (bf16[768,768]{1,0:T(8,128)(2,1)S(1)}, bf16[768,768]{1,0:T(8,128)(2,1)}, u32[]{:S(2)}) copy-start(bf16[768,768]{1,0:T(8,128)(2,1)} %all-gather.12.cloned.1.call-done) | copy-start | bytes 3538948
  474.5 78.5 %reduce-scatter.21.cloned.1.call-start = ((), (), s32[]{:S(2)}) async-start(), calls=%async_computation.15 | async-start | bytes 3932160 | tf_op jit(solution)/shard_map/reduce_scatter | solution.py:184
  474.5 7.2 copy-start.43
  485.8 106.5 %all-gather.18.cloned.1.call-start = ((), (), s32[]{:S(2)}) async-start(), calls=%async_computation.18 | async-start | bytes 3932160 | tf_op jit(solution)/shard_map/all_gather | solution.py:219
  557.0 35.4 %copy-start.17 = (bf16[4,24,8,512]{3,2,0,1:T(8,128)(2,1)S(1)}, bf16[4,24,8,512]{3,2,0,1:T(8,128)(2,1)}, u32[]{:S(2)}) copy-start(bf16[4,24,8,512]{3,2,0,1:T(8,128)(2,1)} %copy-done.16) | copy-start | bytes 2359300
  559.1 338.7 %reduce-scatter.37.cloned.1.call-start = ((), (), s32[]{:S(2)}) async-start(), calls=%async_computation.25 | async-start | bytes 884736
  596.5 313.2 %reduce-scatter.25.cloned.1.call-start = ((), (), s32[]{:S(2)}) async-start(), calls=%async_computation.19 | async-start | bytes 3932160 | tf_op jit(solution)/shard_map/reduce_scatter | solution.py:268
  611.2 7.2 copy-start
  871.8 111.8 %reduce-scatter.29.cloned.1.call-start = ((), (), s32[]{:S(2)}) async-start(), calls=%async_computation.21 | async-start | bytes 2654208 | tf_op jit(solution)/shard_map/reduce_scatter | solution.py:316
  878.8 177.0 %reduce-scatter.27.cloned.1.call-start = ((), (), s32[]{:S(2)}) async-start(), calls=%async_computation.20 | async-start | bytes 2654208 | tf_op jit(solution)/shard_map/reduce_scatter | solution.py:315
  886.6 235.2 %reduce-scatter.35.cloned.1.call-start = ((), (), s32[]{:S(2)}) async-start(), calls=%async_computation.24 | async-start | bytes 884736
  891.8 295.3 %reduce-scatter.33.cloned.1.call-start = ((), (), s32[]{:S(2)}) async-start(), calls=%async_computation.23 | async-start | bytes 884736
  891.9 19.2 %copy-start.2 = (bf16[512,768]{1,0:T(8,128)(2,1)S(1)}, bf16[512,768]{1,0:T(8,128)(2,1)}, u32[]{:S(2)}) copy-start(bf16[512,768]{1,0:T(8,128)(2,1)} %param.22) | copy-start | bytes 2359300
  891.9 19.2 %copy-start.27 = (f32[768]{0:T(1024)S(1)}, f32[768]{0:T(1024)}, u32[]{:S(2)}) copy-start(f32[768]{0:T(1024)} %copy-done.26) | copy-start | bytes 9220
  891.9 19.2 %copy-start.29 = (f32[512]{0:T(512)S(1)}, f32[512]{0:T(512)}, u32[]{:S(2)}) copy-start(f32[512]{0:T(512)} %copy-done.28) | copy-start | bytes 6148
  893.1 359.9 %reduce-scatter.31.cloned.1.call-start = ((), (), s32[]{:S(2)}) async-start(), calls=%async_computation.22 | async-start | bytes 884736
  894.5 18.2 %copy-start.36 = (f32[512]{0:T(512)S(1)}, f32[512]{0:T(512)}, u32[]{:S(2)}) copy-start(f32[512]{0:T(512)} %copy-done.35) | copy-start | bytes 6148
  894.5 18.2 %copy-start.34 = (f32[512]{0:T(512)S(1)}, f32[512]{0:T(512)}, u32[]{:S(2)}) copy-start(f32[512]{0:T(512)} %copy-done.33) | copy-start | bytes 6148
  896.2 18.7 %copy-start.37 = (bf16[768]{0:T(1024)(128)(2,1)S(1)}, bf16[768]{0:T(1024)(128)(2,1)}, u32[]{:S(2)}) copy-start(bf16[768]{0:T(1024)(128)(2,1)} %get-tuple-element.387) | copy-start | bytes 4612
  896.2 18.7 %copy-start.38 = (bf16[768]{0:T(1024)(128)(2,1)S(1)}, bf16[768]{0:T(1024)(128)(2,1)}, u32[]{:S(2)}) copy-start(bf16[768]{0:T(1024)(128)(2,1)} %get-tuple-element.316) | copy-start | bytes 4612
  896.2 72.4 %copy-start.5 = (f32[512,768]{1,0:T(8,128)S(1)}, f32[512,768]{1,0:T(8,128)}, u32[]{:S(2)}) copy-start(f32[512,768]{1,0:T(8,128)} %copy-done.4) | copy-start | bytes 4718596
  909.7 58.9 %copy-start.7 = (bf16[512,768]{1,0:T(8,128)(2,1)S(1)}, bf16[512,768]{1,0:T(8,128)(2,1)}, u32[]{:S(2)}) copy-start(bf16[512,768]{1,0:T(8,128)(2,1)} %reduce-scatter.25.cloned.1.call-done) | copy-start | bytes 2359300
  (26 other events, 82.6 us)
Sparse Core Ops, SparseCore 0:
  61.6 25.7 all-gather.7
  305.6 34.9 reduce-scatter.18
  474.6 37.9 reduce-scatter.22
  514.9 37.9 reduce-scatter.20
Sparse Core Ops, SparseCore 1:
  308.4 38.5 all-gather.11
  349.0 26.8 all-gather.9
  378.2 41.5 all-gather.13
  421.4 26.8 all-gather.15
  559.2 28.3 all-gather.17
  596.6 62.6 reduce-scatter.36
  871.9 37.8 reduce-scatter.24
  914.1 69.4 reduce-scatter.28
  987.9 67.9 reduce-scatter.26
  1060.1 61.6 reduce-scatter.34
  1125.5 61.6 reduce-scatter.32
  1191.4 61.6 reduce-scatter.30
